TPU v7x, 32 devices: a whole 2x2x4 slice. The times are simulated.
32 devices in a mesh: grp: 2 (over x), scan: 16 (over z, y, core).
Axes of the slice: x: 2, y: 2, z: 4, core: 2. Of those that a mesh axis runs over, the one named last changes fastest.
Arguments:
- patterns: bfloat16 [3072, 64, 256], P(('grp', 'scan')), parts along dimension 0, may hold values from -6 to 6
- templates: bfloat16 [32, 64, 256], P('scan'), may hold values from -6 to 6
- radius_bin: int32 [64], replicated, may hold values from 0 to 7
- radial_gain: float32 [8], replicated, may hold values from 0.25 to 4
- orientation: int32 [32, 1], replicated, may hold values from 0 to 15
Outputs:
- corr_map: float32 [3072, 32], P(('grp', 'scan')), parts along dimension 0
- orient_map: float32 [3072, 16], P(('grp', 'scan')), parts along dimension 0
There are 2 independent parts, one for each index of `grp`. A program takes and returns all parts, laid end to end along the dimension named above; an argument that names none is the same for every part. Nothing has to cross between parts.
Inputs may be any that keep to these rules, and one draw needn't show every extreme that they name: Every orientation group holds at least one template.
All inputs are finite; a program needn't handle non-finite values.
Results may differ from a plain program's by a relative error of at most 0.0024.
Values may be sent and summed in bfloat16 or wider, within the bound.
No kernel may reach another device: no remote copies, remote signals or barrier semaphores. Data moves between devices by JAX's collectives and lax.ppermute only.
A program may use at most 128 MiB of HBM per device.

v0:
```python
import math
import jax
import jax.numpy as jnp
from jax import lax
from jax.sharding import PartitionSpec as P

RADII = 64
ANGLES = 256
GAINS = 8
TMPL_PER_GROUP = 2


def with_halo(shard, sides, width):
    for axis, dim in sides:
        size, length = (lax.axis_size(axis), shard.shape[dim])
        up = [(i, (i + 1) % size) for i in range(size - 1)]
        down = [(j, i) for i, j in up]
        last = lax.slice_in_dim(shard, length - width, length, axis=dim)
        leading = lax.slice_in_dim(shard, 0, width, axis=dim)
        before = lax.ppermute(last, axis, up)
        after = lax.ppermute(leading, axis, down)
        shard = jnp.concatenate([before, shard, after], axis=dim)
    return shard


def make_tables():
    half = ANGLES // 2
    along = jnp.arange(ANGLES, dtype=jnp.int32)
    modes = jnp.arange(half + 1, dtype=jnp.int32)
    phase = 2.0 * math.pi / ANGLES * (along[:, None] * modes[None, :] % ANGLES).astype(jnp.float32)
    basis = jnp.concatenate([jnp.cos(phase), jnp.sin(phase[:, 1:half])], axis=1).astype(
        jnp.bfloat16
    )
    factor_norm = 1.0 / (ANGLES * math.sqrt(RADII * ANGLES))
    mode_weight = jnp.where((modes == 0) | (modes == half), 1.0, 2.0).astype(jnp.float32)
    phase_rows = phase.T
    inverse = jnp.concatenate(
        [mode_weight[:, None] * jnp.cos(phase_rows), -mode_weight[:, None] * jnp.sin(phase_rows)],
        axis=0,
    )
    return (basis, (inverse * factor_norm).astype(jnp.bfloat16))


def spectrum(raw, basis):
    count = raw.shape[0]
    flat = raw.reshape(-1, ANGLES)
    spec = lax.dot_general(
        basis, flat, (((0,), (1,)), ((), ())), preferred_element_type=jnp.float32
    )
    return spec.reshape(ANGLES, count, RADII)


def mode_products(left, right):
    return jnp.einsum("kpr,ktr->ktp", left, right, preferred_element_type=jnp.float32)


def correlate(pat_spec, tmpl_spec, inverse):
    half = ANGLES // 2
    count = tmpl_spec.shape[1]
    pos_count = pat_spec.shape[1]
    pat_cos = pat_spec[: half + 1]
    pat_sin = pat_spec[half + 1 :]
    tmpl_cos = tmpl_spec[: half + 1]
    tmpl_sin = tmpl_spec[half + 1 :]
    both_cos = mode_products(pat_cos, tmpl_cos)
    both_sin = mode_products(pat_sin, tmpl_sin)
    cos_sin = mode_products(pat_cos[1:half], tmpl_sin)
    sin_cos = mode_products(pat_sin, tmpl_cos[1:half])
    edge = jnp.zeros((1, count, pos_count), jnp.float32)
    real_part = both_cos + jnp.concatenate([edge, both_sin, edge], axis=0)
    imag_part = jnp.concatenate([edge, cos_sin - sin_cos, edge], axis=0)
    cross = jnp.concatenate([real_part, imag_part], axis=0).astype(jnp.bfloat16)
    cross = cross.reshape(2 * (half + 1), count * pos_count)
    shifted = lax.dot_general(
        inverse, cross, (((0,), (0,)), ((), ())), preferred_element_type=jnp.float32
    )
    return jnp.max(shifted, axis=0).reshape(count, pos_count)


def block_of(count, limit):
    size = limit
    while size > 1:
        if count % size == 0:
            return size
        size = size // 2
    return 1


def correlate_into(carry, pat_spec, count, prepare, inverse):
    block_size = block_of(count, 64)

    def step(index, total):
        begin = index * block_size
        values = correlate(pat_spec, prepare(begin, block_size), inverse)
        return lax.dynamic_update_slice(total, values, (begin, jnp.int32(0)))

    return lax.fori_loop(0, count // block_size, step, carry)


def on_device(patterns, templates, radius_bin, radial_gain, orientation):
    basis, inverse = make_tables()
    pos_count = patterns.shape[0]
    total_tmpl = templates.shape[0] * lax.axis_size("scan")
    group_count = total_tmpl // TMPL_PER_GROUP
    onehot = (radius_bin[:, None] == jnp.arange(GAINS, dtype=jnp.int32)[None, :]).astype(
        jnp.float32
    )
    radius_weight = jnp.sum(onehot * radial_gain[None, :], axis=1)
    pat_spec = (spectrum(patterns, basis) * radius_weight[None, None, :]).astype(jnp.bfloat16)
    initial = jnp.zeros((total_tmpl, pos_count), jnp.float32)

    def raw_rows(piece):
        return lambda begin, size: spectrum(
            lax.dynamic_slice_in_dim(piece, begin, size, 0), basis
        ).astype(jnp.bfloat16)

    piece = lax.all_gather(templates, "scan", axis=0, tiled=True)
    by_template = correlate_into(initial, pat_spec, piece.shape[0], raw_rows(piece), inverse)
    corr_map = by_template.T
    groups = orientation[:, 0]
    member = groups[None, :] == jnp.arange(group_count, dtype=jnp.int32)[:, None]
    group_block = block_of(group_count, 16)
    member_blocks = member.reshape(group_count // group_block, group_block, total_tmpl)

    def group_max(mask):
        return jnp.max(jnp.where(mask[:, :, None], by_template[None, :, :], -jnp.inf), axis=1)

    best = lax.map(group_max, member_blocks).reshape(group_count, pos_count).T
    padded = with_halo(best, (("scan", 0),), 1)
    orient_map = 0.25 * (padded[:-2] + 2.0 * best + padded[2:])
    return (corr_map, orient_map)


def solution(mesh):
    placed = (P(("grp", "scan"), None, None), P("scan", None, None), P(), P(), P())
    return jax.shard_map(
        on_device,
        mesh=mesh,
        in_specs=placed,
        out_specs=(P(("grp", "scan"), None), P(("grp", "scan"), None)),
        check_vma=False,
    )
```

profile of v0, /device:TPU:5, one launch (start us, length us, event | category | flops | bytes accessed | tf_op | source)
XLA Modules:
  0.0 101.3 jit_solution(18244889343172042133)
XLA Ops:
  7.2 0.0 copy-start
  7.2 0.0 all-gather.2.cloned.1.call-start
  7.2 0.7 all-gather.2.cloned.1.call-update
  7.9 1.0 select_reduce_fusion.1
  8.9 1.0 cosine_convert_fusion
  9.8 0.1 fusion.19
  10.0 0.5 fusion.31
  10.5 0.0 copy-done
  10.5 3.6 %multiply_convert_fusion = bf16[256,96,64]{0,1,2:T(8,128)(2,1)S(1)} fusion(f32[64]{0:T(128)S(1)} %select_reduce_fusion.1, bf16[96,64,256]{2,1,0:T(8,128)(2,1)S(1)} %copy-done, bf16[256,127]{1,0:T(8,128)(2,1)S(1)} %fusion.31, bf16[256,129]{1,0:T(8,128)(2,1)S(1)} %cosine_convert_fusion), kind=kOutput, calls=%fused_computation | convolution fusion | flops 808714240 | bytes 6422784 | tf_op jit(solution)/shard_map/dot_general | solution.py:47
  14.1 0.0 copy-start.2
  14.1 2.7 %fusion.41 = (bf16[127,96,64]{0,1,2:T(8,128)(2,1)}, bf16[127,96,64]{0,1,2:T(8,128)(2,1)}) fusion(bf16[256,96,64]{0,1,2:T(8,128)(2,1)S(1)} %multiply_convert_fusion), kind=kLoop, calls=%fused_computation.59 | loop fusion | bytes 6242304 | tf_op jit(solution)/shard_map/while/body/eval_jaxpr/slice | solution.py:62
  16.9 0.0 copy-done.2
  16.9 4.0 %copy.44 = bf16[127,96,64]{1,2,0:T(8,128)(2,1)} copy(bf16[127,96,64]{0,1,2:T(8,128)(2,1)} %get-tuple-element.28) | data formatting | bytes 3121152 | tf_op jit(solution)/shard_map/while/body/eval_jaxpr/slice | solution.py:67
  20.9 4.0 %copy.42 = bf16[127,96,64]{1,2,0:T(8,128)(2,1)} copy(bf16[127,96,64]{0,1,2:T(8,128)(2,1)} %get-tuple-element.20) | data formatting | bytes 3121152 | tf_op jit(solution)/shard_map/while/body/eval_jaxpr/slice | solution.py:62
  24.9 0.0 copy-start.8
  24.9 5.0 %copy.40 = bf16[129,96,64]{1,2,0:T(8,128)(2,1)} copy(bf16[129,96,64]{0,1,2:T(8,128)(2,1)} %bitcast.19) | data formatting | bytes 3170304 | tf_op jit(solution)/shard_map/while/body/eval_jaxpr/slice | solution.py:61
  29.8 0.0 copy-done.8
  29.9 1.2 %sine_multiply_fusion = (f32[129,256]{1,0:T(8,128)S(1)}, f32[129,256]{1,0:T(8,128)}) fusion(f32[129]{0:T(256)S(1)} %fusion.35, f32[129]{0:T(256)S(1)} %or_select_fusion), kind=kLoop, calls=%fused_computation.35 | loop fusion | flops 528384 | bytes 265224 | tf_op jit(solution)/shard_map/mul | solution.py:38
  31.1 17.7 %all-gather.2.cloned.1.call-done = bf16[32,64,256]{2,1,0:T(8,128)(2,1)} async-done(((bf16[2,64,256]{2,1,0:T(8,128)(2,1)}), bf16[32,64,256]{2,1,0:T(8,128)(2,1)}) %all-gather.2.cloned.1.call-update) | async-done | bytes 1048592 | tf_op jit(solution)/shard_map/all_gather | solution.py:117
  48.8 1.7 %convolution_convert_fusion = bf16[256,32,64]{0,2,1:T(8,128)(2,1)S(1)} fusion(bf16[32,64,256]{2,1,0:T(8,128)(2,1)} %all-gather.2.cloned.1.call-done, bf16[256,127]{1,0:T(8,128)(2,1)S(1)} %fusion.31, bf16[256,129]{1,0:T(8,128)(2,1)S(1)} %cosine_convert_fusion), kind=kOutput, calls=%fused_computation.14 | convolution fusion | flops 269221888 | bytes 2228224 | tf_op jit(solution)/shard_map/while/body/eval_jaxpr/dot_general | solution.py:47
  50.6 0.0 copy-start.3
  50.6 0.9 copy-done.3
  51.5 1.4 %fusion.42 = (bf16[127,32,64]{0,2,1:T(8,128)(2,1)}, bf16[127,32,64]{0,2,1:T(8,128)(2,1)}) fusion(bf16[256,32,64]{0,2,1:T(8,128)(2,1)S(1)} %convolution_convert_fusion), kind=kLoop, calls=%fused_computation.60 | loop fusion | bytes 2080768 | tf_op jit(solution)/shard_map/while/body/eval_jaxpr/slice | solution.py:68
  52.9 3.5 %copy.41 = bf16[127,32,64]{2,1,0:T(8,128)(2,1)} copy(bf16[127,32,64]{0,2,1:T(8,128)(2,1)} %get-tuple-element.30) | data formatting | bytes 1040384 | tf_op jit(solution)/shard_map/while/body/eval_jaxpr/slice | solution.py:64
  56.4 3.5 %copy.45 = bf16[127,32,64]{2,1,0:T(8,128)(2,1)} copy(bf16[127,32,64]{0,2,1:T(8,128)(2,1)} %get-tuple-element.29) | data formatting | bytes 1040384 | tf_op jit(solution)/shard_map/while/body/eval_jaxpr/slice | solution.py:68
  59.9 0.0 copy-start.1
  59.9 2.7 %fusion.45 = f32[127,32,96]{2,1,0:T(8,128)S(1)} fusion(bf16[127,32,64]{2,1,0:T(8,128)(2,1)} %copy.41, bf16[127,96,64]{1,2,0:T(8,128)(2,1)} %copy.44), kind=kOutput, calls=%fused_computation.63 | convolution fusion | flops 49938432 | bytes 3641344 | tf_op jit(solution)/shard_map/while/body/eval_jaxpr/kpr,ktr->ktp/dot_general | solution.py:54
  62.6 0.0 copy-done.1
  62.6 0.1 copy-done.4
  62.7 2.0 %fusion.44 = f32[127,32,96]{2,1,0:T(8,128)} fusion(bf16[127,32,64]{2,1,0:T(8,128)(2,1)S(1)} %copy-done.4, bf16[127,96,64]{1,2,0:T(8,128)(2,1)S(1)} %copy-done.1), kind=kOutput, calls=%fused_computation.62 | convolution fusion | flops 49938432 | bytes 3641344 | tf_op jit(solution)/shard_map/while/body/eval_jaxpr/kpr,ktr->ktp/dot_general | solution.py:54
  64.7 0.0 copy-done.5
  64.7 1.7 %subtract_convert_fusion = bf16[127,32,96]{2,1,0:T(8,128)(2,1)} fusion(f32[127,32,96]{2,1,0:T(8,128)S(1)} %fusion.45, bf16[127,32,64]{2,1,0:T(8,128)(2,1)S(1)} %copy-done.5, bf16[127,96,64]{1,2,0:T(8,128)(2,1)S(1)} %copy-done.1), kind=kOutput, calls=%fused_computation.5 | convolution fusion | flops 50718720 | bytes 4421632 | tf_op jit(solution)/shard_map/while/body/eval_jaxpr/kpr,ktr->ktp/dot_general | solution.py:54
  66.4 2.7 %copy.47 = bf16[127,32,96]{0,2,1:T(8,128)(2,1)} copy(bf16[127,32,96]{2,1,0:T(8,128)(2,1)} %subtract_convert_fusion) | data formatting | bytes 1560576 | tf_op jit(solution)/shard_map/convert.4
  69.1 2.4 %copy.48 = bf16[127,3072]{1,0:T(8,128)(2,1)} copy(bf16[127,3072]{0,1:T(8,128)(2,1)} %bitcast.21) | data formatting | bytes 1560576 | tf_op jit(solution)/shard_map/while/body/eval_jaxpr/concatenate | solution.py:72
  71.5 2.8 %copy.39 = bf16[129,32,64]{2,1,0:T(8,128)(2,1)} copy(bf16[129,32,64]{0,2,1:T(8,128)(2,1)} %bitcast.20) | data formatting | bytes 1056768 | tf_op jit(solution)/shard_map/while/body/eval_jaxpr/slice | solution.py:63
  74.3 4.3 %fusion.4 = bf16[129,32,96]{2,1,0:T(8,128)(2,1)} fusion(f32[1,32,96]{2,1,0:T(8,128)S(1)} %broadcast.63, f32[127,32,96]{2,1,0:T(8,128)} %fusion.44, bf16[129,32,64]{2,1,0:T(8,128)(2,1)} %copy.39, bf16[129,96,64]{1,2,0:T(8,128)(2,1)} %copy.40), kind=kOutput, calls=%fused_computation.4 | convolution fusion | flops 52310016 | bytes 4478976 | tf_op jit(solution)/shard_map/while/body/eval_jaxpr/kpr,ktr->ktp/dot_general | solution.py:54
  78.6 3.4 %concatenate.33 = bf16[129,3072]{1,0:T(8,128)(2,1)} reshape(bf16[129,32,96]{2,1,0:T(8,128)(2,1)} %fusion.4) | data formatting | bytes 1585152 | tf_op jit(solution)/shard_map/while/body/eval_jaxpr/concatenate | solution.py:72
  81.9 0.0 copy-done.6
  82.0 2.5 %fusion.13 = f32[3072]{0:T(1024)S(1)} fusion(bf16[1,3072]{1,0:T(2,128)(2,1)S(1)} %concatenate.34, bf16[127,3072]{1,0:T(8,128)(2,1)} %copy.48, bf16[129,3072]{1,0:T(8,128)(2,1)} %concatenate.33, f32[129,256]{1,0:T(8,128)S(1)} %get-tuple-element.37, f32[129,256]{1,0:T(8,128)S(1)} %copy-done.6), kind=kOutput, calls=%fused_computation.15 | convolution fusion | flops 413121024 | bytes 1855488 | tf_op jit(solution)/shard_map/while/body/eval_jaxpr/dot_general | solution.py:74
  84.4 0.1 reshape.51
  84.5 0.1 select_reduce_fusion
  84.6 0.1 fusion.43
  84.7 3.2 %collective-permute-start = (f32[1,16]{0,1:T(8,128)S(1)}, f32[1,16]{0,1:T(8,128)S(1)}, u32[]{:S(2)}, u32[]{:S(2)}) collective-permute-start(f32[1,16]{0,1:T(8,128)S(1)} %get-tuple-element.31), channel_id=1, source_target_pairs={{0,1},{1,2},{2,3},{3,4},{4,5},{5,6},{6,7},{7,8},{8,9},{9,10},{10,1... | collective-permute-start | bytes 200 | tf_op jit(solution)/shard_map/ppermute | solution.py:20
  87.9 1.9 %collective-permute-start.1 = (f32[1,16]{0,1:T(8,128)S(1)}, f32[1,16]{0,1:T(8,128)S(1)}, u32[]{:S(2)}, u32[]{:S(2)}) collective-permute-start(f32[1,16]{0,1:T(8,128)S(1)} %get-tuple-element.36), channel_id=1, source_target_pairs={{1,0},{2,1},{3,2},{4,3},{5,4},{6,5},{7,6},{8,7},{9,8},{10,9},{11,1... | collective-permute-start | bytes 200 | tf_op jit(solution)/shard_map/ppermute | solution.py:21
  89.9 0.0 collective-permute-done
  89.9 3.9 %collective-permute-done.1 = f32[1,16]{0,1:T(8,128)S(1)} collective-permute-done((f32[1,16]{0,1:T(8,128)S(1)}, f32[1,16]{0,1:T(8,128)S(1)}, u32[]{:S(2)}, u32[]{:S(2)}) %collective-permute-start.1) | collective-permute-done | bytes 96 | tf_op jit(solution)/shard_map/ppermute | solution.py:21
  93.8 0.7 fusion.33
  94.5 0.0 copy-done.7
  (9 shorter events, 0.0 us)
Async XLA Ops:
  7.2 3.3 %copy-start = (bf16[96,64,256]{2,1,0:T(8,128)(2,1)S(1)}, bf16[96,64,256]{2,1,0:T(8,128)(2,1)}, u32[]{:S(2)}) copy-start(bf16[96,64,256]{2,1,0:T(8,128)(2,1)} %param.5) | copy-start | bytes 9437188
  7.2 41.6 %all-gather.2.cloned.1.call-start = ((), (), s32[]{:S(2)}) async-start(), calls=%async_computation | async-start | bytes 1114112 | tf_op jit(solution)/shard_map/all_gather | solution.py:117
  14.1 2.7 %copy-start.2 = (bf16[256,96,64]{0,1,2:T(8,128)(2,1)}, bf16[256,96,64]{0,1,2:T(8,128)(2,1)S(1)}, u32[]{:S(2)}) copy-start(bf16[256,96,64]{0,1,2:T(8,128)(2,1)S(1)} %multiply_convert_fusion) | copy-start | bytes 9437188
  24.9 5.0 %copy-start.8 = (s32[32,1]{0,1:T(1,128)S(1)}, s32[32,1]{0,1:T(1,128)}, u32[]{:S(2)}) copy-start(s32[32,1]{0,1:T(1,128)} %param.9) | copy-start | bytes 388
  50.6 1.0 copy-start.3
  59.9 2.7 %copy-start.1 = (bf16[127,96,64]{1,2,0:T(8,128)(2,1)S(1)}, bf16[127,96,64]{1,2,0:T(8,128)(2,1)}, u32[]{:S(2)}) copy-start(bf16[127,96,64]{1,2,0:T(8,128)(2,1)} %copy.42) | copy-start | bytes 4681732
  59.9 2.8 %copy-start.4 = (bf16[127,32,64]{2,1,0:T(8,128)(2,1)S(1)}, bf16[127,32,64]{2,1,0:T(8,128)(2,1)}, u32[]{:S(2)}) copy-start(bf16[127,32,64]{2,1,0:T(8,128)(2,1)} %copy.41) | copy-start | bytes 1560580
  62.7 2.0 %copy-start.5 = (bf16[127,32,64]{2,1,0:T(8,128)(2,1)S(1)}, bf16[127,32,64]{2,1,0:T(8,128)(2,1)}, u32[]{:S(2)}) copy-start(bf16[127,32,64]{2,1,0:T(8,128)(2,1)} %copy.45) | copy-start | bytes 1560580
  74.3 7.6 %copy-start.6 = (f32[129,256]{1,0:T(8,128)S(1)}, f32[129,256]{1,0:T(8,128)}, u32[]{:S(2)}) copy-start(f32[129,256]{1,0:T(8,128)} %get-tuple-element.38) | copy-start | bytes 396292
  84.5 10.0 %copy-start.7 = (f32[32,96]{1,0:T(8,128)}, f32[32,96]{1,0:T(8,128)S(1)}, u32[]{:S(2)}) copy-start(f32[32,96]{1,0:T(8,128)S(1)} %reshape.51) | copy-start | bytes 36868
  84.7 5.2 %collective-permute-start = (f32[1,16]{0,1:T(8,128)S(1)}, f32[1,16]{0,1:T(8,128)S(1)}, u32[]{:S(2)}, u32[]{:S(2)}) collective-permute-start(f32[1,16]{0,1:T(8,128)S(1)} %get-tuple-element.31), channel_id=1, source_target_pairs={{0,1},{1,2},{2,3},{3,4},{4,5},{5,6},{6,7},{7,8},{8,9},{9,10},{10,1... | collective-permute-start | bytes 200 | tf_op jit(solution)/shard_map/ppermute | solution.py:20
  87.9 5.9 %collective-permute-start.1 = (f32[1,16]{0,1:T(8,128)S(1)}, f32[1,16]{0,1:T(8,128)S(1)}, u32[]{:S(2)}, u32[]{:S(2)}) collective-permute-start(f32[1,16]{0,1:T(8,128)S(1)} %get-tuple-element.36), channel_id=1, source_target_pairs={{1,0},{2,1},{3,2},{4,3},{5,4},{6,5},{7,6},{8,7},{9,8},{10,9},{11,1... | collective-permute-start | bytes 200 | tf_op jit(solution)/shard_map/ppermute | solution.py:21
Sparse Core Ops, SparseCore 0:
  10.2 38.5 all-gather.1
where the time goes:
time: 102 us; the launch traced here: 101 us
  local copies, waits for them, and re-layouts  36.6 us (36%)
  waiting for transfers between devices  22.3 us (22%)
  matrix products  18.5 us (18%)
  between operations  14.2 us (14%)
  starting transfers between devices  5.19 us (5%)
  other arithmetic  4.61 us (5%)
    all_gather x1, waiting for transfers between devices, on_device(): piece = lax.all_gather(templates, 'scan', axis=0, tiled=True)  17.7 us
    dot_general x4, matrix products, mode_products(): jnp.einsum('kpr,ktr->ktp', left, right, preferred_element_type=jnp.float32)  10.6 us
    slice x2, local copies, waits for them, and re-layouts, correlate(): pat_sin = pat_spec[half + 1:]  6.72 us
    concatenate x3, local copies, waits for them, and re-layouts, correlate(): cross = jnp.concatenate([real_part, imag_part], axis=0).astype(jnp.bfloat16)  5.75 us
    dot_general x2, matrix products, spectrum(): lax.dot_general(basis, flat, (((0,), (1,)), ((), ())), preferred_element_...  5.37 us
    slice x1, local copies, waits for them, and re-layouts, correlate(): pat_cos = pat_spec[:half + 1]  4.96 us
    slice x2, local copies, waits for them, and re-layouts, correlate(): sin_cos = mode_products(pat_sin, tmpl_cos[1:half])  4.9 us
    slice x1, local copies, waits for them, and re-layouts, correlate(): cos_sin = mode_products(pat_cos[1:half], tmpl_sin)  4 us
  transfers between devices with their start and end apart: 3, of which 2 were waited for; matrix products, arithmetic and copies ran while one was open for 23% of the time, Pallas kernels for 0%

commit v1 on v0

--- a/solution.py
+++ b/solution.py
@@ -114,7 +114,33 @@
             lax.dynamic_slice_in_dim(piece, begin, size, 0), basis
         ).astype(jnp.bfloat16)
 
-    piece = lax.all_gather(templates, "scan", axis=0, tiled=True)
+    side_arr, back, m_next = (
+        lax.psum(1, axis_name="scan"),
+        lax.axis_index("scan"),
+        templates.shape[0],
+    )
+    row_list = []
+    for idx in range(side_arr):
+        row_list.append((idx, (idx + 1) % side_arr))
+    by_rank = []
+    for idx in range(side_arr):
+        by_rank.append((idx, (idx - 1) % side_arr))
+    piece = jnp.zeros(
+        (*templates.shape[:0], side_arr * m_next, *templates.shape[1:]), templates.dtype
+    )
+    piece = lax.dynamic_update_slice_in_dim(piece, templates, back * m_next, axis=0)
+    res = inter = templates
+    carry_in = side_arr // 2
+    for nth in range(1, carry_in + 1):
+        res = lax.ppermute(res, axis_name="scan", perm=row_list)
+        piece = lax.dynamic_update_slice_in_dim(
+            piece, res, (back - nth) % side_arr * m_next, axis=0
+        )
+        if nth < side_arr - carry_in:
+            inter = lax.ppermute(inter, axis_name="scan", perm=by_rank)
+            piece = lax.dynamic_update_slice_in_dim(
+                piece, inter, (back + nth) % side_arr * m_next, axis=0
+            )
     by_template = correlate_into(initial, pat_spec, piece.shape[0], raw_rows(piece), inverse)
     corr_map = by_template.T
     groups = orientation[:, 0]

time: 102 us -> 117 us (1.15)
  the two profiles are of different devices: /device:TPU:5 before, /device:TPU:0 now
where the time goes in v1:
time: 117 us; the launch traced here: 116 us
  local copies, waits for them, and re-layouts  38.5 us (33%)
  starting transfers between devices  36.7 us (31%)
  matrix products  17.2 us (15%)
  waiting for transfers between devices  17.1 us (15%)
  other arithmetic  5.58 us (5%)
    ppermute x7, starting transfers between devices, on_device(): inter = lax.ppermute(inter, axis_name='scan', perm=by_rank)  31.8 us
    ppermute x8, waiting for transfers between devices, on_device(): res = lax.ppermute(res, axis_name='scan', perm=row_list)  16.1 us
    dot_general x4, matrix products, mode_products(): jnp.einsum('kpr,ktr->ktp', left, right, preferred_element_type=jnp.float32)  10.6 us
    slice x2, local copies, waits for them, and re-layouts, correlate(): pat_sin = pat_spec[half + 1:]  6.71 us
    concatenate x3, local copies, waits for them, and re-layouts, correlate(): cross = jnp.concatenate([real_part, imag_part], axis=0).astype(jnp.bfloat16)  5.73 us
    slice x1, local copies, waits for them, and re-layouts, correlate(): pat_cos = pat_spec[:half + 1]  4.99 us
    slice x2, local copies, waits for them, and re-layouts, correlate(): sin_cos = mode_products(pat_sin, tmpl_cos[1:half])  4.86 us
    dot_general x2, matrix products, spectrum(): lax.dot_general(basis, flat, (((0,), (1,)), ((), ())), preferred_element_...  4.14 us
  transfers between devices with their start and end apart: 17, of which 8 were waited for; matrix products, arithmetic and copies ran while one was open for 22% of the time, Pallas kernels for 0%

profile of v1, /device:TPU:0, one launch (start us, length us, event | category | flops | bytes accessed | tf_op | source)
XLA Modules:
  0.0 116.0 jit_solution(3415660139846758389)
XLA Ops:
  0.6 0.5 collective-permute-start
  1.1 5.1 %collective-permute-start.1 = (bf16[2,64,256]{2,1,0:T(8,128)(2,1)}, bf16[2,64,256]{2,1,0:T(8,128)(2,1)}, u32[]{:S(2)}, u32[]{:S(2)}) collective-permute-start(bf16[2,64,256]{2,1,0:T(8,128)(2,1)} %param.6), channel_id=1, source_target_pairs={{0,15},{1,0},{2,1},{3,2},{4,3},{5,4},{6,5},{7,6},{8,7},{9,8},{10,9... | collective-permute-start | bytes 196616 | tf_op jit(solution)/shard_map/ppermute | solution.py:140
  6.2 0.1 fusion.19
  6.3 1.0 cosine_convert_fusion
  7.3 0.5 fusion.31
  7.8 0.8 select_reduce_fusion.1
  8.6 3.6 %multiply_convert_fusion = bf16[256,96,64]{0,1,2:T(8,128)(2,1)S(1)} fusion(f32[64]{0:T(128)S(1)} %select_reduce_fusion.1, bf16[96,64,256]{2,1,0:T(8,128)(2,1)S(1)} %copy-done, bf16[256,127]{1,0:T(8,128)(2,1)S(1)} %fusion.31, bf16[256,129]{1,0:T(8,128)(2,1)S(1)} %cosine_convert_fusion), kind=kOutput, calls=%fused_computation | convolution fusion | flops 808714240 | bytes 6422784 | tf_op jit(solution)/shard_map/dot_general | solution.py:47
  12.2 2.7 %fusion.41 = (bf16[127,96,64]{0,1,2:T(8,128)(2,1)}, bf16[127,96,64]{0,1,2:T(8,128)(2,1)}) fusion(bf16[256,96,64]{0,1,2:T(8,128)(2,1)S(1)} %multiply_convert_fusion), kind=kLoop, calls=%fused_computation.75 | loop fusion | bytes 6242304 | tf_op jit(solution)/shard_map/while/body/eval_jaxpr/slice | solution.py:62
  15.0 4.0 %copy.33 = bf16[127,96,64]{1,2,0:T(8,128)(2,1)} copy(bf16[127,96,64]{0,1,2:T(8,128)(2,1)} %get-tuple-element.28) | data formatting | bytes 3121152 | tf_op jit(solution)/shard_map/while/body/eval_jaxpr/slice | solution.py:67
  19.0 4.0 %copy.31 = bf16[127,96,64]{1,2,0:T(8,128)(2,1)} copy(bf16[127,96,64]{0,1,2:T(8,128)(2,1)} %get-tuple-element.20) | data formatting | bytes 3121152 | tf_op jit(solution)/shard_map/while/body/eval_jaxpr/slice | solution.py:62
  23.0 5.0 %copy.29 = bf16[129,96,64]{1,2,0:T(8,128)(2,1)} copy(bf16[129,96,64]{0,1,2:T(8,128)(2,1)} %bitcast.19) | data formatting | bytes 3170304 | tf_op jit(solution)/shard_map/while/body/eval_jaxpr/slice | solution.py:61
  28.0 0.5 sine_multiply_fusion
  28.5 1.2 %cosine_multiply_fusion = f32[129,256]{1,0:T(8,128)} fusion(f32[129]{0:T(256)S(1)} %get-tuple-element.37), kind=kLoop, calls=%fused_computation.36 | loop fusion | flops 495360 | bytes 132612 | tf_op jit(solution)/shard_map/mul | solution.py:38
  29.7 0.7 iota_compare_fusion
  30.6 4.4 %collective-permute-start.3 = (bf16[2,64,256]{2,1,0:T(8,128)(2,1)}, bf16[2,64,256]{2,1,0:T(8,128)(2,1)S(1)}, u32[]{:S(2)}, u32[]{:S(2)}) collective-permute-start(bf16[2,64,256]{2,1,0:T(8,128)(2,1)} %collective-permute-done.1), channel_id=1, source_target_pairs={{0,15},{1,0},{2,1},{3,2},{4,3},{5,4},{6,5},{7,6},{8,7},{9,8},{10,9... | collective-permute-start | bytes 196616 | tf_op jit(solution)/shard_map/ppermute | solution.py:140
  35.0 0.8 constant_dynamic-update-slice_fusion.14
  35.8 0.8 constant_dynamic-update-slice_fusion.13
  36.7 0.5 collective-permute-done.2
  37.2 4.4 %collective-permute-start.5 = (bf16[2,64,256]{2,1,0:T(8,128)(2,1)S(1)}, bf16[2,64,256]{2,1,0:T(8,128)(2,1)S(1)}, u32[]{:S(2)}, u32[]{:S(2)}) collective-permute-start(bf16[2,64,256]{2,1,0:T(8,128)(2,1)S(1)} %collective-permute-done.3), channel_id=1, source_target_pairs={{0,15},{1,0},{2,1},{3,2},{4,3},{5,4},{6,5},{7,6},{8,7},{9,8},{10,9... | collective-permute-start | bytes 196616 | tf_op jit(solution)/shard_map/ppermute | solution.py:140
  41.7 1.9 %collective-permute-done.4 = bf16[2,64,256]{2,1,0:T(8,128)(2,1)S(1)} collective-permute-done((bf16[2,64,256]{2,1,0:T(8,128)(2,1)S(1)}, bf16[2,64,256]{2,1,0:T(8,128)(2,1)S(1)}, u32[]{:S(2)}, u32[]{:S(2)}) %collective-permute-start.4) | collective-permute-done | bytes 65568 | tf_op jit(solution)/shard_map/ppermute | solution.py:135
  43.6 4.5 %collective-permute-start.7 = (bf16[2,64,256]{2,1,0:T(8,128)(2,1)S(1)}, bf16[2,64,256]{2,1,0:T(8,128)(2,1)S(1)}, u32[]{:S(2)}, u32[]{:S(2)}) collective-permute-start(bf16[2,64,256]{2,1,0:T(8,128)(2,1)S(1)} %collective-permute-done.5), channel_id=1, source_target_pairs={{0,15},{1,0},{2,1},{3,2},{4,3},{5,4},{6,5},{7,6},{8,7},{9,8},{10,9... | collective-permute-start | bytes 196616 | tf_op jit(solution)/shard_map/ppermute | solution.py:140
  48.1 1.9 %collective-permute-done.6 = bf16[2,64,256]{2,1,0:T(8,128)(2,1)S(1)} collective-permute-done((bf16[2,64,256]{2,1,0:T(8,128)(2,1)S(1)}, bf16[2,64,256]{2,1,0:T(8,128)(2,1)S(1)}, u32[]{:S(2)}, u32[]{:S(2)}) %collective-permute-start.6) | collective-permute-done | bytes 65568 | tf_op jit(solution)/shard_map/ppermute | solution.py:135
  50.0 4.5 %collective-permute-start.9 = (bf16[2,64,256]{2,1,0:T(8,128)(2,1)S(1)}, bf16[2,64,256]{2,1,0:T(8,128)(2,1)S(1)}, u32[]{:S(2)}, u32[]{:S(2)}) collective-permute-start(bf16[2,64,256]{2,1,0:T(8,128)(2,1)S(1)} %collective-permute-done.7), channel_id=1, source_target_pairs={{0,15},{1,0},{2,1},{3,2},{4,3},{5,4},{6,5},{7,6},{8,7},{9,8},{10,9... | collective-permute-start | bytes 196616 | tf_op jit(solution)/shard_map/ppermute | solution.py:140
  54.5 1.9 %collective-permute-done.8 = bf16[2,64,256]{2,1,0:T(8,128)(2,1)S(1)} collective-permute-done((bf16[2,64,256]{2,1,0:T(8,128)(2,1)S(1)}, bf16[2,64,256]{2,1,0:T(8,128)(2,1)S(1)}, u32[]{:S(2)}, u32[]{:S(2)}) %collective-permute-start.8) | collective-permute-done | bytes 65568 | tf_op jit(solution)/shard_map/ppermute | solution.py:135
  56.4 4.5 %collective-permute-start.11 = (bf16[2,64,256]{2,1,0:T(8,128)(2,1)S(1)}, bf16[2,64,256]{2,1,0:T(8,128)(2,1)S(1)}, u32[]{:S(2)}, u32[]{:S(2)}) collective-permute-start(bf16[2,64,256]{2,1,0:T(8,128)(2,1)S(1)} %collective-permute-done.9), channel_id=1, source_target_pairs={{0,15},{1,0},{2,1},{3,2},{4,3},{5,4},{6,5},{7,6},{8,7},{9,8},{10,9... | collective-permute-start | bytes 196616 | tf_op jit(solution)/shard_map/ppermute | solution.py:140
  60.9 1.9 %collective-permute-done.10 = bf16[2,64,256]{2,1,0:T(8,128)(2,1)S(1)} collective-permute-done((bf16[2,64,256]{2,1,0:T(8,128)(2,1)S(1)}, bf16[2,64,256]{2,1,0:T(8,128)(2,1)S(1)}, u32[]{:S(2)}, u32[]{:S(2)}) %collective-permute-start.10) | collective-permute-done | bytes 65568 | tf_op jit(solution)/shard_map/ppermute | solution.py:135
  62.8 4.5 %collective-permute-start.13 = (bf16[2,64,256]{2,1,0:T(8,128)(2,1)S(1)}, bf16[2,64,256]{2,1,0:T(8,128)(2,1)S(1)}, u32[]{:S(2)}, u32[]{:S(2)}) collective-permute-start(bf16[2,64,256]{2,1,0:T(8,128)(2,1)S(1)} %collective-permute-done.11), channel_id=1, source_target_pairs={{0,15},{1,0},{2,1},{3,2},{4,3},{5,4},{6,5},{7,6},{8,7},{9,8},{10,9... | collective-permute-start | bytes 196616 | tf_op jit(solution)/shard_map/ppermute | solution.py:140
  67.3 1.9 %collective-permute-done.12 = bf16[2,64,256]{2,1,0:T(8,128)(2,1)S(1)} collective-permute-done((bf16[2,64,256]{2,1,0:T(8,128)(2,1)S(1)}, bf16[2,64,256]{2,1,0:T(8,128)(2,1)S(1)}, u32[]{:S(2)}, u32[]{:S(2)}) %collective-permute-start.12) | collective-permute-done | bytes 65568 | tf_op jit(solution)/shard_map/ppermute | solution.py:135
  69.2 6.3 %collective-permute-done.14 = bf16[2,64,256]{2,1,0:T(8,128)(2,1)S(1)} collective-permute-done((bf16[2,64,256]{2,1,0:T(8,128)(2,1)S(1)}, bf16[2,64,256]{2,1,0:T(8,128)(2,1)S(1)}, u32[]{:S(2)}, u32[]{:S(2)}) %collective-permute-start.14) | collective-permute-done | bytes 65568 | tf_op jit(solution)/shard_map/ppermute | solution.py:135
  75.5 0.5 convolution_convert_fusion
  76.0 1.0 copy-done.3
  77.0 1.4 %fusion.42 = (bf16[127,32,64]{0,2,1:T(8,128)(2,1)}, bf16[127,32,64]{0,2,1:T(8,128)(2,1)}) fusion(bf16[256,32,64]{0,2,1:T(8,128)(2,1)S(1)} %convolution_convert_fusion), kind=kLoop, calls=%fused_computation.76 | loop fusion | bytes 2080768 | tf_op jit(solution)/shard_map/while/body/eval_jaxpr/slice | solution.py:68
  78.4 3.5 %copy.30 = bf16[127,32,64]{2,1,0:T(8,128)(2,1)} copy(bf16[127,32,64]{0,2,1:T(8,128)(2,1)} %get-tuple-element.30) | data formatting | bytes 1040384 | tf_op jit(solution)/shard_map/while/body/eval_jaxpr/slice | solution.py:64
  81.9 3.5 %copy.34 = bf16[127,32,64]{2,1,0:T(8,128)(2,1)} copy(bf16[127,32,64]{0,2,1:T(8,128)(2,1)} %get-tuple-element.29) | data formatting | bytes 1040384 | tf_op jit(solution)/shard_map/while/body/eval_jaxpr/slice | solution.py:68
  85.4 2.7 %fusion.45 = f32[127,32,96]{2,1,0:T(8,128)S(1)} fusion(bf16[127,32,64]{2,1,0:T(8,128)(2,1)} %copy.30, bf16[127,96,64]{1,2,0:T(8,128)(2,1)} %copy.33), kind=kOutput, calls=%fused_computation.79 | convolution fusion | flops 49938432 | bytes 3641344 | tf_op jit(solution)/shard_map/while/body/eval_jaxpr/kpr,ktr->ktp/dot_general | solution.py:54
  88.2 2.0 %fusion.44 = f32[127,32,96]{2,1,0:T(8,128)} fusion(bf16[127,32,64]{2,1,0:T(8,128)(2,1)S(1)} %copy-done.4, bf16[127,96,64]{1,2,0:T(8,128)(2,1)S(1)} %copy-done.1), kind=kOutput, calls=%fused_computation.78 | convolution fusion | flops 49938432 | bytes 3641344 | tf_op jit(solution)/shard_map/while/body/eval_jaxpr/kpr,ktr->ktp/dot_general | solution.py:54
  90.2 1.6 %subtract_convert_fusion = bf16[127,32,96]{2,1,0:T(8,128)(2,1)} fusion(f32[127,32,96]{2,1,0:T(8,128)S(1)} %fusion.45, bf16[127,32,64]{2,1,0:T(8,128)(2,1)S(1)} %copy-done.5, bf16[127,96,64]{1,2,0:T(8,128)(2,1)S(1)} %copy-done.1), kind=kOutput, calls=%fused_computation.5 | convolution fusion | flops 50718720 | bytes 4421632 | tf_op jit(solution)/shard_map/while/body/eval_jaxpr/kpr,ktr->ktp/dot_general | solution.py:54
  91.8 2.7 %copy.36 = bf16[127,32,96]{0,2,1:T(8,128)(2,1)} copy(bf16[127,32,96]{2,1,0:T(8,128)(2,1)} %subtract_convert_fusion) | data formatting | bytes 1560576 | tf_op jit(solution)/shard_map/convert.4
  94.6 2.4 %copy.37 = bf16[127,3072]{1,0:T(8,128)(2,1)} copy(bf16[127,3072]{0,1:T(8,128)(2,1)} %bitcast.21) | data formatting | bytes 1560576 | tf_op jit(solution)/shard_map/while/body/eval_jaxpr/concatenate | solution.py:72
  96.9 2.9 %copy.28 = bf16[129,32,64]{2,1,0:T(8,128)(2,1)} copy(bf16[129,32,64]{0,2,1:T(8,128)(2,1)} %bitcast.20) | data formatting | bytes 1056768 | tf_op jit(solution)/shard_map/while/body/eval_jaxpr/slice | solution.py:63
  99.8 4.3 %fusion.4 = bf16[129,32,96]{2,1,0:T(8,128)(2,1)} fusion(f32[1,32,96]{2,1,0:T(8,128)S(1)} %broadcast.78, f32[127,32,96]{2,1,0:T(8,128)} %fusion.44, bf16[129,32,64]{2,1,0:T(8,128)(2,1)} %copy.28, bf16[129,96,64]{1,2,0:T(8,128)(2,1)} %copy.29), kind=kOutput, calls=%fused_computation.4 | convolution fusion | flops 52310016 | bytes 4478976 | tf_op jit(solution)/shard_map/while/body/eval_jaxpr/kpr,ktr->ktp/dot_general | solution.py:54
  104.0 3.4 %concatenate.33 = bf16[129,3072]{1,0:T(8,128)(2,1)} reshape(bf16[129,32,96]{2,1,0:T(8,128)(2,1)} %fusion.4) | data formatting | bytes 1585152 | tf_op jit(solution)/shard_map/while/body/eval_jaxpr/concatenate | solution.py:72
  107.4 2.5 %fusion.13 = f32[3072]{0:T(1024)S(1)} fusion(bf16[1,3072]{1,0:T(2,128)(2,1)S(1)} %concatenate.34, bf16[127,3072]{1,0:T(8,128)(2,1)} %copy.37, bf16[129,3072]{1,0:T(8,128)(2,1)} %concatenate.33, f32[129,256]{1,0:T(8,128)S(1)} %sine_multiply_fusion, f32[129,256]{1,0:T(8,128)S(1)} %copy-done.6), kind=kOutput, calls=%fused_computation.15 | convolution fusion | flops 413121024 | bytes 1855488 | tf_op jit(solution)/shard_map/while/body/eval_jaxpr/dot_general | solution.py:74
  110.0 0.1 select_reduce_fusion
  110.2 1.3 %collective-permute-start.16 = (f32[1,16]{0,1:T(8,128)S(1)}, f32[1,16]{0,1:T(8,128)S(1)}, u32[]{:S(2)}, u32[]{:S(2)}) collective-permute-start(f32[1,16]{0,1:T(8,128)S(1)} %get-tuple-element.36), channel_id=1, source_target_pairs={{1,0},{2,1},{3,2},{4,3},{5,4},{6,5},{7,6},{8,7},{9,8},{10,9},{11,1... | collective-permute-start | bytes 200 | tf_op jit(solution)/shard_map/ppermute | solution.py:21
  111.5 3.0 %collective-permute-start.15 = (f32[1,16]{0,1:T(8,128)S(1)}, f32[1,16]{0,1:T(8,128)S(1)}, u32[]{:S(2)}, u32[]{:S(2)}) collective-permute-start(f32[1,16]{0,1:T(8,128)S(1)} %get-tuple-element.31), channel_id=1, source_target_pairs={{0,1},{1,2},{2,3},{3,4},{4,5},{5,6},{6,7},{7,8},{8,9},{9,10},{10,1... | collective-permute-start | bytes 200 | tf_op jit(solution)/shard_map/ppermute | solution.py:20
  114.5 0.8 collective-permute-done.15
  115.3 0.7 fusion.33
  (53 shorter events, 0.7 us)
Async XLA Ops:
  0.6 8.0 %copy-start = (bf16[96,64,256]{2,1,0:T(8,128)(2,1)S(1)}, bf16[96,64,256]{2,1,0:T(8,128)(2,1)}, u32[]{:S(2)}) copy-start(bf16[96,64,256]{2,1,0:T(8,128)(2,1)} %param.5) | copy-start | bytes 9437188
  0.6 29.9 %collective-permute-start = (bf16[2,64,256]{2,1,0:T(8,128)(2,1)}, bf16[2,64,256]{2,1,0:T(8,128)(2,1)}, u32[]{:S(2)}, u32[]{:S(2)}) collective-permute-start(bf16[2,64,256]{2,1,0:T(8,128)(2,1)} %param.6), channel_id=1, source_target_pairs={{0,1},{1,2},{2,3},{3,4},{4,5},{5,6},{6,7},{7,8},{8,9},{9,10},{10,1... | collective-permute-start | bytes 196616 | tf_op jit(solution)/shard_map/ppermute | solution.py:135
  1.1 29.4 %collective-permute-start.1 = (bf16[2,64,256]{2,1,0:T(8,128)(2,1)}, bf16[2,64,256]{2,1,0:T(8,128)(2,1)}, u32[]{:S(2)}, u32[]{:S(2)}) collective-permute-start(bf16[2,64,256]{2,1,0:T(8,128)(2,1)} %param.6), channel_id=1, source_target_pairs={{0,15},{1,0},{2,1},{3,2},{4,3},{5,4},{6,5},{7,6},{8,7},{9,8},{10,9... | collective-permute-start | bytes 196616 | tf_op jit(solution)/shard_map/ppermute | solution.py:140
  12.2 2.7 %copy-start.2 = (bf16[256,96,64]{0,1,2:T(8,128)(2,1)}, bf16[256,96,64]{0,1,2:T(8,128)(2,1)S(1)}, u32[]{:S(2)}) copy-start(bf16[256,96,64]{0,1,2:T(8,128)(2,1)S(1)} %multiply_convert_fusion) | copy-start | bytes 9437188
  23.0 7.5 %copy-start.7 = (bf16[2,64,256]{2,1,0:T(8,128)(2,1)S(1)}, bf16[2,64,256]{2,1,0:T(8,128)(2,1)}, u32[]{:S(2)}) copy-start(bf16[2,64,256]{2,1,0:T(8,128)(2,1)} %param.6) | copy-start | bytes 196612
  30.5 6.7 %collective-permute-start.2 = (bf16[2,64,256]{2,1,0:T(8,128)(2,1)}, bf16[2,64,256]{2,1,0:T(8,128)(2,1)S(1)}, u32[]{:S(2)}, u32[]{:S(2)}) collective-permute-start(bf16[2,64,256]{2,1,0:T(8,128)(2,1)} %collective-permute-done), channel_id=1, source_target_pairs={{0,1},{1,2},{2,3},{3,4},{4,5},{5,6},{6,7},{7,8},{8,9},{9,10},{10,1... | collective-permute-start | bytes 196616 | tf_op jit(solution)/shard_map/ppermute | solution.py:135
  30.6 6.6 %collective-permute-start.3 = (bf16[2,64,256]{2,1,0:T(8,128)(2,1)}, bf16[2,64,256]{2,1,0:T(8,128)(2,1)S(1)}, u32[]{:S(2)}, u32[]{:S(2)}) collective-permute-start(bf16[2,64,256]{2,1,0:T(8,128)(2,1)} %collective-permute-done.1), channel_id=1, source_target_pairs={{0,15},{1,0},{2,1},{3,2},{4,3},{5,4},{6,5},{7,6},{8,7},{9,8},{10,9... | collective-permute-start | bytes 196616 | tf_op jit(solution)/shard_map/ppermute | solution.py:140
  37.2 6.4 %collective-permute-start.4 = (bf16[2,64,256]{2,1,0:T(8,128)(2,1)S(1)}, bf16[2,64,256]{2,1,0:T(8,128)(2,1)S(1)}, u32[]{:S(2)}, u32[]{:S(2)}) collective-permute-start(bf16[2,64,256]{2,1,0:T(8,128)(2,1)S(1)} %collective-permute-done.2), channel_id=1, source_target_pairs={{0,1},{1,2},{2,3},{3,4},{4,5},{5,6},{6,7},{7,8},{8,9},{9,10},{10,1... | collective-permute-start | bytes 196616 | tf_op jit(solution)/shard_map/ppermute | solution.py:135
  37.2 6.3 %collective-permute-start.5 = (bf16[2,64,256]{2,1,0:T(8,128)(2,1)S(1)}, bf16[2,64,256]{2,1,0:T(8,128)(2,1)S(1)}, u32[]{:S(2)}, u32[]{:S(2)}) collective-permute-start(bf16[2,64,256]{2,1,0:T(8,128)(2,1)S(1)} %collective-permute-done.3), channel_id=1, source_target_pairs={{0,15},{1,0},{2,1},{3,2},{4,3},{5,4},{6,5},{7,6},{8,7},{9,8},{10,9... | collective-permute-start | bytes 196616 | tf_op jit(solution)/shard_map/ppermute | solution.py:140
  43.6 6.4 %collective-permute-start.6 = (bf16[2,64,256]{2,1,0:T(8,128)(2,1)S(1)}, bf16[2,64,256]{2,1,0:T(8,128)(2,1)S(1)}, u32[]{:S(2)}, u32[]{:S(2)}) collective-permute-start(bf16[2,64,256]{2,1,0:T(8,128)(2,1)S(1)} %collective-permute-done.4), channel_id=1, source_target_pairs={{0,1},{1,2},{2,3},{3,4},{4,5},{5,6},{6,7},{7,8},{8,9},{9,10},{10,1... | collective-permute-start | bytes 196616 | tf_op jit(solution)/shard_map/ppermute | solution.py:135
  43.6 6.4 %collective-permute-start.7 = (bf16[2,64,256]{2,1,0:T(8,128)(2,1)S(1)}, bf16[2,64,256]{2,1,0:T(8,128)(2,1)S(1)}, u32[]{:S(2)}, u32[]{:S(2)}) collective-permute-start(bf16[2,64,256]{2,1,0:T(8,128)(2,1)S(1)} %collective-permute-done.5), channel_id=1, source_target_pairs={{0,15},{1,0},{2,1},{3,2},{4,3},{5,4},{6,5},{7,6},{8,7},{9,8},{10,9... | collective-permute-start | bytes 196616 | tf_op jit(solution)/shard_map/ppermute | solution.py:140
  50.0 6.4 %collective-permute-start.8 = (bf16[2,64,256]{2,1,0:T(8,128)(2,1)S(1)}, bf16[2,64,256]{2,1,0:T(8,128)(2,1)S(1)}, u32[]{:S(2)}, u32[]{:S(2)}) collective-permute-start(bf16[2,64,256]{2,1,0:T(8,128)(2,1)S(1)} %collective-permute-done.6), channel_id=1, source_target_pairs={{0,1},{1,2},{2,3},{3,4},{4,5},{5,6},{6,7},{7,8},{8,9},{9,10},{10,1... | collective-permute-start | bytes 196616 | tf_op jit(solution)/shard_map/ppermute | solution.py:135
  50.0 6.4 %collective-permute-start.9 = (bf16[2,64,256]{2,1,0:T(8,128)(2,1)S(1)}, bf16[2,64,256]{2,1,0:T(8,128)(2,1)S(1)}, u32[]{:S(2)}, u32[]{:S(2)}) collective-permute-start(bf16[2,64,256]{2,1,0:T(8,128)(2,1)S(1)} %collective-permute-done.7), channel_id=1, source_target_pairs={{0,15},{1,0},{2,1},{3,2},{4,3},{5,4},{6,5},{7,6},{8,7},{9,8},{10,9... | collective-permute-start | bytes 196616 | tf_op jit(solution)/shard_map/ppermute | solution.py:140
  56.3 6.4 %collective-permute-start.10 = (bf16[2,64,256]{2,1,0:T(8,128)(2,1)S(1)}, bf16[2,64,256]{2,1,0:T(8,128)(2,1)S(1)}, u32[]{:S(2)}, u32[]{:S(2)}) collective-permute-start(bf16[2,64,256]{2,1,0:T(8,128)(2,1)S(1)} %collective-permute-done.8), channel_id=1, source_target_pairs={{0,1},{1,2},{2,3},{3,4},{4,5},{5,6},{6,7},{7,8},{8,9},{9,10},{10,1... | collective-permute-start | bytes 196616 | tf_op jit(solution)/shard_map/ppermute | solution.py:135
  56.4 6.4 %collective-permute-start.11 = (bf16[2,64,256]{2,1,0:T(8,128)(2,1)S(1)}, bf16[2,64,256]{2,1,0:T(8,128)(2,1)S(1)}, u32[]{:S(2)}, u32[]{:S(2)}) collective-permute-start(bf16[2,64,256]{2,1,0:T(8,128)(2,1)S(1)} %collective-permute-done.9), channel_id=1, source_target_pairs={{0,15},{1,0},{2,1},{3,2},{4,3},{5,4},{6,5},{7,6},{8,7},{9,8},{10,9... | collective-permute-start | bytes 196616 | tf_op jit(solution)/shard_map/ppermute | solution.py:140
  62.7 6.4 %collective-permute-start.12 = (bf16[2,64,256]{2,1,0:T(8,128)(2,1)S(1)}, bf16[2,64,256]{2,1,0:T(8,128)(2,1)S(1)}, u32[]{:S(2)}, u32[]{:S(2)}) collective-permute-start(bf16[2,64,256]{2,1,0:T(8,128)(2,1)S(1)} %collective-permute-done.10), channel_id=1, source_target_pairs={{0,1},{1,2},{2,3},{3,4},{4,5},{5,6},{6,7},{7,8},{8,9},{9,10},{10,1... | collective-permute-start | bytes 196616 | tf_op jit(solution)/shard_map/ppermute | solution.py:135
  62.8 6.4 %collective-permute-start.13 = (bf16[2,64,256]{2,1,0:T(8,128)(2,1)S(1)}, bf16[2,64,256]{2,1,0:T(8,128)(2,1)S(1)}, u32[]{:S(2)}, u32[]{:S(2)}) collective-permute-start(bf16[2,64,256]{2,1,0:T(8,128)(2,1)S(1)} %collective-permute-done.11), channel_id=1, source_target_pairs={{0,15},{1,0},{2,1},{3,2},{4,3},{5,4},{6,5},{7,6},{8,7},{9,8},{10,9... | collective-permute-start | bytes 196616 | tf_op jit(solution)/shard_map/ppermute | solution.py:140
  69.1 6.4 %collective-permute-start.14 = (bf16[2,64,256]{2,1,0:T(8,128)(2,1)S(1)}, bf16[2,64,256]{2,1,0:T(8,128)(2,1)S(1)}, u32[]{:S(2)}, u32[]{:S(2)}) collective-permute-start(bf16[2,64,256]{2,1,0:T(8,128)(2,1)S(1)} %collective-permute-done.12), channel_id=1, source_target_pairs={{0,1},{1,2},{2,3},{3,4},{4,5},{5,6},{6,7},{7,8},{8,9},{9,10},{10,1... | collective-permute-start | bytes 196616 | tf_op jit(solution)/shard_map/ppermute | solution.py:135
  76.0 1.0 copy-start.3
  85.4 2.7 %copy-start.1 = (bf16[127,96,64]{1,2,0:T(8,128)(2,1)S(1)}, bf16[127,96,64]{1,2,0:T(8,128)(2,1)}, u32[]{:S(2)}) copy-start(bf16[127,96,64]{1,2,0:T(8,128)(2,1)} %copy.31) | copy-start | bytes 4681732
  85.4 2.8 %copy-start.4 = (bf16[127,32,64]{2,1,0:T(8,128)(2,1)S(1)}, bf16[127,32,64]{2,1,0:T(8,128)(2,1)}, u32[]{:S(2)}) copy-start(bf16[127,32,64]{2,1,0:T(8,128)(2,1)} %copy.30) | copy-start | bytes 1560580
  88.2 2.0 %copy-start.5 = (bf16[127,32,64]{2,1,0:T(8,128)(2,1)S(1)}, bf16[127,32,64]{2,1,0:T(8,128)(2,1)}, u32[]{:S(2)}) copy-start(bf16[127,32,64]{2,1,0:T(8,128)(2,1)} %copy.34) | copy-start | bytes 1560580
  99.8 7.6 %copy-start.6 = (f32[129,256]{1,0:T(8,128)S(1)}, f32[129,256]{1,0:T(8,128)}, u32[]{:S(2)}) copy-start(f32[129,256]{1,0:T(8,128)} %cosine_multiply_fusion) | copy-start | bytes 396292
  109.9 6.1 %copy-start.8 = (f32[32,96]{1,0:T(8,128)}, f32[32,96]{1,0:T(8,128)S(1)}, u32[]{:S(2)}) copy-start(f32[32,96]{1,0:T(8,128)S(1)} %reshape.51) | copy-start | bytes 36868
  110.2 4.3 %collective-permute-start.16 = (f32[1,16]{0,1:T(8,128)S(1)}, f32[1,16]{0,1:T(8,128)S(1)}, u32[]{:S(2)}, u32[]{:S(2)}) collective-permute-start(f32[1,16]{0,1:T(8,128)S(1)} %get-tuple-element.36), channel_id=1, source_target_pairs={{1,0},{2,1},{3,2},{4,3},{5,4},{6,5},{7,6},{8,7},{9,8},{10,9},{11,1... | collective-permute-start | bytes 200 | tf_op jit(solution)/shard_map/ppermute | solution.py:21
  111.5 3.8 %collective-permute-start.15 = (f32[1,16]{0,1:T(8,128)S(1)}, f32[1,16]{0,1:T(8,128)S(1)}, u32[]{:S(2)}, u32[]{:S(2)}) collective-permute-start(f32[1,16]{0,1:T(8,128)S(1)} %get-tuple-element.31), channel_id=1, source_target_pairs={{0,1},{1,2},{2,3},{3,4},{4,5},{5,6},{6,7},{7,8},{8,9},{9,10},{10,1... | collective-permute-start | bytes 200 | tf_op jit(solution)/shard_map/ppermute | solution.py:20
